TPU v7x, 32 devices: a whole 2x2x4 slice. The times are simulated.
32 devices in a mesh: hst: 8 (over y, x, core), local: 4 (over z).
Axes of the slice: x: 2, y: 2, z: 4, core: 2. Of those that a mesh axis runs over, the one named last changes fastest.
Arguments:
- image_feats: bfloat16 [4096, 1152], P(('hst', 'local')), may hold values from -6 to 6
- text_feats: bfloat16 [4096, 1152], P(('hst', 'local')), may hold values from -6 to 6
- image_proj: bfloat16 [1152, 1152], replicated, may hold values from -0.1875 to 0.1875
- text_proj: bfloat16 [1152, 1152], replicated, may hold values from -0.1875 to 0.1875
- scale: float32 [1], replicated, may hold values from 4 to 16
- bias: float32 [1], replicated, may hold values from -4 to -2
Outputs:
- image_grad: float32 [4096, 1152], P(('hst', 'local'))
- text_grad: float32 [4096, 1152], P(('hst', 'local'))
All inputs are finite; a program needn't handle non-finite values.
Results may differ from a plain program's by a relative error of at most 0.005.
Values may be sent and summed in bfloat16 or wider, within the bound.
A program may use at most 64 MiB of HBM per device.

v0:
```python
import functools

import jax
import jax.numpy as jnp
from jax import lax
from jax.experimental import pallas as pl
from jax.experimental.pallas import tpu as pltpu
from jax.sharding import PartitionSpec as P

GROUP_DEVS = 8
CHUNKS = 2
BACK_CHUNKS = 2
SIBLING, PARTNER, RELAY, BACK = range(4)


def flipped(member, bit):
    return member + bit - 2 * bit * lax.rem(lax.div(member, bit), 2)


def kernel(
    axis_sizes,
    image_feats,
    text_feats,
    image_proj,
    text_proj,
    knobs,
    image_grad,
    text_grad,
    feats,
    away_feats,
    proj,
    proj_t,
    emb,
    unit,
    recip,
    own_sum,
    away_sum,
    away_out,
    away_in,
    load_sem,
    send_sem,
    recv_sem,
):
    hosts, locals_ = axis_sizes
    stride = hosts * locals_ // GROUP_DEVS
    position = lax.axis_index("hst") * locals_ + lax.axis_index("local")
    member = lax.div(position, stride)
    rest = lax.rem(position, stride)

    def device_of(other):
        place = other * stride + rest
        return (lax.div(place, locals_), lax.rem(place, locals_))

    sibling = device_of(flipped(member, 1))
    partners = (device_of(flipped(member, 2)), device_of(flipped(member, 4)))

    rows = image_feats.shape[0]
    part = rows // CHUNKS
    feat_loads = []
    proj_loads = []
    for side, (feat_ref, proj_ref) in enumerate(
        ((image_feats, image_proj), (text_feats, text_proj))
    ):
        feat_loads.append(
            pltpu.make_async_copy(feat_ref, feats.at[side], load_sem.at[side, 0])
        )
        proj_loads.append(
            pltpu.make_async_copy(proj_ref, proj.at[side], load_sem.at[side, 1])
        )
        feat_loads[side].start()
        proj_loads[side].start()

    barrier = pltpu.get_barrier_semaphore()
    for other in (sibling,) + partners:
        pl.semaphore_signal(
            barrier, inc=1, device_id=other, device_id_type=pl.DeviceIdType.MESH
        )

    def remote(src, dst, kind, side, piece, device):
        return pltpu.make_async_remote_copy(
            src_ref=src,
            dst_ref=dst,
            send_sem=send_sem.at[kind, side, piece],
            recv_sem=recv_sem.at[kind, side, piece],
            device_id=device,
            device_id_type=pl.DeviceIdType.MESH,
        )

    copies = {}
    given = (image_feats, text_feats)

    def send(kind, side, piece):
        size = rows // (BACK_CHUNKS if kind == BACK else CHUNKS)
        span = pl.ds(piece * size, size)
        if kind == SIBLING:
            src, dst, device = emb.at[side, 0, span], emb.at[side, 1, span], sibling
        elif kind == PARTNER:
            src, dst, device = given[side].at[span], away_feats.at[side, span], partners[side]
        elif kind == RELAY:
            src, dst, device = emb.at[side, 2, span], emb.at[side, 3, span], sibling
        else:
            src, dst, device = away_out.at[side, span], away_in.at[side, span], partners[side]
        copy = remote(src, dst, kind, side, piece, device)
        copy.start()
        copies[kind, side, piece] = copy

    pl.semaphore_wait(barrier, 3)
    for piece in range(CHUNKS):
        for side in range(2):
            send(PARTNER, side, piece)

    def embed(rows_in, side):
        raw = jnp.dot(rows_in, proj[side], preferred_element_type=jnp.float32)
        inverse = lax.rsqrt(jnp.sum(raw * raw, axis=1, keepdims=True) + 1e-06)
        return raw * inverse, inverse

    for side in range(2):
        feat_loads[side].wait()
        proj_loads[side].wait()
        normal, inverse = embed(feats[side], side)
        unit[side] = normal
        recip[side] = inverse
        emb[side, 0] = normal.astype(jnp.bfloat16)
        for piece in range(CHUNKS):
            send(SIBLING, side, piece)

    temper = knobs[0:1, 0:1]
    offset = knobs[1:2, 0:1]

    def pull(side, row_slot, span, first, last):
        mine = emb[side, row_slot, span]
        theirs = emb[1 - side, first:last].reshape((last - first) * rows, mine.shape[1])
        logits = temper * lax.dot_general(
            mine, theirs, (((1,), (1,)), ((), ())), preferred_element_type=jnp.float32
        ) + offset
        slope = jax.nn.sigmoid(logits)
        if row_slot == 0 and first == 0:
            down = lax.broadcasted_iota(jnp.int32, slope.shape, 0)
            along = lax.broadcasted_iota(jnp.int32, slope.shape, 1)
            slope = slope - jnp.where(down == along, 1.0, 0.0)
        return jnp.dot(
            slope.astype(jnp.bfloat16), theirs, preferred_element_type=jnp.float32
        )

    whole = pl.ds(0, rows)
    for side in range(2):
        for piece in range(CHUNKS):
            copies[SIBLING, side, piece].wait_recv()
    for side in range(2):
        own_sum[side] = pull(side, 0, whole, 0, 2)

    for piece in range(CHUNKS):
        span = pl.ds(piece * part, part)
        for side in range(2):
            copies[PARTNER, side, piece].wait_recv()
            emb[side, 2, span] = embed(away_feats[side, span], side)[0].astype(jnp.bfloat16)
            send(RELAY, side, piece)
        for side in (1, 0):
            away_sum[side, span] = pull(side, 2, span, 0, 2)
    for side in (1, 0):
        away_sum[side] += pull(side, 2, whole, 2, 3)

    for side in (1, 0):
        for piece in range(CHUNKS):
            copies[RELAY, 1 - side, piece].wait_recv()
        away_out[side] = (away_sum[side] + pull(side, 2, whole, 3, 4)).astype(jnp.bfloat16)
        for piece in range(BACK_CHUNKS):
            send(BACK, side, piece)
    for side in (1, 0):
        own_sum[side] += pull(side, 0, whole, 2, 4)
    for side in (1, 0):
        proj_t[side] = proj[side].T

    outs = (image_grad, text_grad)
    part = rows // BACK_CHUNKS
    for piece in range(BACK_CHUNKS):
        span = pl.ds(piece * part, part)
        for side in (1, 0):
            copies[BACK, side, piece].wait_recv()
            slope = temper * (own_sum[side, span] + away_in[side, span].astype(jnp.float32))
            normal = unit[side, span]
            inner = jnp.sum(normal * slope, axis=1, keepdims=True)
            down = (recip[side, span] * (slope - normal * inner)).astype(jnp.bfloat16)
            outs[side][span] = jnp.dot(
                down, proj_t[side], preferred_element_type=jnp.float32
            )

    for copy in copies.values():
        copy.wait_send()


def on_device(axis_sizes, image_feats, text_feats, image_proj, text_proj, scale, bias):
    rows, width = image_feats.shape
    embed = image_proj.shape[1]
    out = jax.ShapeDtypeStruct((rows, width), jnp.float32)
    anywhere = pl.BlockSpec(memory_space=pltpu.HBM)
    vmem = pl.BlockSpec(memory_space=pltpu.VMEM)
    return pl.pallas_call(
        functools.partial(kernel, axis_sizes),
        out_shape=(out, out),
        in_specs=[anywhere] * 4 + [vmem],
        out_specs=(vmem, vmem),
        scratch_shapes=[
            pltpu.VMEM((2, rows, width), jnp.bfloat16),
            pltpu.VMEM((2, rows, width), jnp.bfloat16),
            pltpu.VMEM((2, width, embed), jnp.bfloat16),
            pltpu.VMEM((2, embed, width), jnp.bfloat16),
            pltpu.VMEM((2, 4, rows, embed), jnp.bfloat16),
            pltpu.VMEM((2, rows, embed), jnp.float32),
            pltpu.VMEM((2, rows, 1), jnp.float32),
            pltpu.VMEM((2, rows, embed), jnp.float32),
            pltpu.VMEM((2, rows, embed), jnp.float32),
            pltpu.VMEM((2, rows, embed), jnp.bfloat16),
            pltpu.VMEM((2, rows, embed), jnp.bfloat16),
            pltpu.SemaphoreType.DMA((2, 2)),
            pltpu.SemaphoreType.DMA((4, 2, max(CHUNKS, BACK_CHUNKS))),
            pltpu.SemaphoreType.DMA((4, 2, max(CHUNKS, BACK_CHUNKS))),
        ],
        compiler_params=pltpu.CompilerParams(
            collective_id=0, has_side_effects=True, vmem_limit_bytes=52428800
        ),
    )(
        *(pltpu.with_memory_space_constraint(x, pltpu.HBM) for x in (image_feats, text_feats, image_proj, text_proj)), jnp.broadcast_to(jnp.stack([scale, bias]), (2, 128))
    )


def solution(mesh):
    in_specs = (P(("hst", "local"), None), P(("hst", "local"), None), P(), P(), P(), P())
    out_specs = (P(("hst", "local"), None), P(("hst", "local"), None))
    axis_sizes = (mesh.shape["hst"], mesh.shape["local"])
    return jax.shard_map(
        functools.partial(on_device, axis_sizes),
        mesh=mesh,
        in_specs=in_specs,
        out_specs=out_specs,
        check_vma=False,
    )
```

profile of v0, /device:TPU:0, one launch (start us, length us, event | category | flops | bytes accessed | tf_op | source)
XLA Modules:
  0.0 28.4 jit_solution(5596951025211898507)
XLA Ops:
  1.9 0.1 maximum_bitcast_fusion
  2.0 0.1 broadcast_in_dim.8.knobs
  2.1 24.7 %shard_map.77 = (f32[128,1152]{1,0:T(8,128)S(1)}, f32[128,1152]{1,0:T(8,128)S(1)}) custom-call(bf16[128,1152]{1,0:T(8,128)(2,1)} %image_feats.1, bf16[128,1152]{1,0:T(8,128)(2,1)} %text_feats.1, bf16[1152,1152]{1,0:T(8,128)(2,1)} %image_proj.1, bf16[1152,1152]{1,0:T(8,128)(2,1)} %text_proj.1, f32[2,128]{1,0:T(2,128)S(1)} %broadcast_in_dim.8.knobs), custom_call_target="tpu_custom_call" | custom-call | tf_op jit(solution)/shard_map/pallas_call | solution.py:198
  26.8 0.8 %copy.12 = f32[128,1152]{1,0:T(8,128)} copy(f32[128,1152]{1,0:T(8,128)S(1)} %get-tuple-element.4) | data formatting | bytes 1179648
  27.6 0.8 %copy.13 = f32[128,1152]{1,0:T(8,128)} copy(f32[128,1152]{1,0:T(8,128)S(1)} %get-tuple-element.5) | data formatting | bytes 1179648
where the time goes:
time: 28.6 us; the launch traced here: 28.4 us
  Pallas kernels  24.7 us (86%)
  between operations  1.93 us (7%)
  local copies, waits for them, and re-layouts  1.7 us (6%)
    pallas_call x1, Pallas kernels, on_device(): pl.pallas_call(functools.partial(kernel, axis_sizes), out_shape=(out, out...  24.7 us
    unnamed x2, local copies, waits for them, and re-layouts  1.63 us

commit v1 on v0

v1 whole, which is shorter than its diff:
```python
import functools

import jax
import jax.numpy as jnp
from jax import lax
from jax.experimental import pallas as pl
from jax.experimental.pallas import tpu as pltpu
from jax.sharding import PartitionSpec as P

GROUP_DEVS = 8
EARLY, LATE = 0, 1
OWN, SIB, AWAY, FAR = range(4)
RAW_PART = (1, 2)
LATE_PARTS = (2, 1, 1)
EARLY_BACK = (1, 1)
LATE_BACK = (2, 1, 1)


def flipped(member, bit):
    return member + bit - 2 * bit * lax.rem(lax.div(member, bit), 2)


def spans_of(rows, parts):
    total, at, out = sum(parts), 0, []
    for part in parts:
        size = rows * part // total
        out.append((at, size))
        at += size
    return out


def place_of(axis_sizes):
    hosts, locals_ = axis_sizes
    stride = hosts * locals_ // GROUP_DEVS
    position = lax.axis_index("hst") * locals_ + lax.axis_index("local")
    return lax.div(position, stride), lax.rem(position, stride), stride


def kernel(
    axis_sizes,
    image_feats,
    text_feats,
    image_proj,
    text_proj,
    scale,
    bias,
    done,
    last,
    late_proj_t,
    feats,
    away_feats,
    proj,
    early_proj_t,
    emb,
    unit,
    recip,
    own_sum,
    away_sum,
    away_out,
    away_in,
    temper_ref,
    offset_ref,
    load_sem,
    send_sem,
    recv_sem,
):
    member, rest, stride = place_of(axis_sizes)
    role = lax.rem(member, 2)
    locals_ = axis_sizes[1]

    def device_of(other):
        place = other * stride + rest
        return (lax.div(place, locals_), lax.rem(place, locals_))

    sibling = device_of(flipped(member, 1))
    image_partner = flipped(member, 2)
    text_partner = flipped(member, 4)
    partners = (
        device_of(text_partner * (1 - role) + image_partner * role),
        device_of(image_partner * (1 - role) + text_partner * role),
    )
    rows = image_feats.shape[0]

    def loads(early, late):
        copies = []
        for slot, (feat_ref, proj_ref) in enumerate((early, late)):
            copies.append(
                (
                    pltpu.make_async_copy(feat_ref, feats.at[slot], load_sem.at[slot, 0]),
                    pltpu.make_async_copy(proj_ref, proj.at[slot], load_sem.at[slot, 1]),
                )
            )
        return copies

    image, text = (image_feats, image_proj), (text_feats, text_proj)
    for which, (early, late) in enumerate(((text, image), (image, text))):

        @pl.when(role == which)
        def _():
            given = loads(early, late)
            for kind in range(2):
                for slot in range(2):
                    given[slot][kind].start()

    loaded = loads(image, text)
    knob_loads = [
        pltpu.make_async_copy(given, held, load_sem.at[2, i])
        for i, (given, held) in enumerate(((scale, temper_ref), (bias, offset_ref)))
    ]
    for copy in knob_loads:
        copy.start()

    barrier = pltpu.get_barrier_semaphore()
    for other in (sibling,) + partners:
        pl.semaphore_signal(
            barrier, inc=1, device_id=other, device_id_type=pl.DeviceIdType.MESH
        )

    copies = {}

    def send(name, src, dst, device):
        index = len(copies)
        copy = pltpu.make_async_remote_copy(
            src_ref=src,
            dst_ref=dst,
            send_sem=send_sem.at[index],
            recv_sem=recv_sem.at[index],
            device_id=device,
            device_id_type=pl.DeviceIdType.MESH,
        )
        copy.start()
        copies[name] = copy

    def embed(rows_in, side):
        raw = jnp.dot(rows_in, proj[side], preferred_element_type=jnp.float32)
        inverse = lax.rsqrt(jnp.sum(raw * raw, axis=1, keepdims=True) + 1e-06)
        return raw * inverse, inverse

    def embed_own(side):
        loaded[side][1].wait()
        normal, inverse = embed(feats[side], side)
        unit[side] = normal
        recip[side] = inverse
        emb[side, OWN] = normal.astype(jnp.bfloat16)

    raw_rows = rows * RAW_PART[0] // RAW_PART[1]
    raw_span, emb_span = pl.ds(0, raw_rows), pl.ds(raw_rows, rows - raw_rows)
    late_spans = [pl.ds(*s) for s in spans_of(rows, LATE_PARTS)]
    back_spans = [
        [pl.ds(*s) for s in spans_of(rows, parts)] for parts in (EARLY_BACK, LATE_BACK)
    ]
    whole = pl.ds(0, rows)

    loaded[EARLY][0].wait()
    loaded[LATE][0].wait()
    pl.semaphore_wait(barrier, 3)
    send("raw", feats.at[EARLY, raw_span], away_feats.at[raw_span], partners[EARLY])
    embed_own(EARLY)
    send(
        "early",
        emb.at[EARLY, OWN, emb_span],
        emb.at[EARLY, AWAY, emb_span],
        partners[EARLY],
    )
    send("sib early", emb.at[EARLY, OWN], emb.at[LATE, SIB], sibling)
    embed_own(LATE)
    for i, span in enumerate(late_spans):
        send(("late", i), emb.at[LATE, OWN, span], emb.at[LATE, AWAY, span], partners[LATE])
    send("sib late", emb.at[LATE, OWN], emb.at[EARLY, SIB], sibling)

    for copy in knob_loads:
        copy.wait()
    temper = temper_ref[0]
    offset = offset_ref[0]

    def pull(mine, theirs, own=False):
        logits = temper * lax.dot_general(
            mine, theirs, (((1,), (1,)), ((), ())), preferred_element_type=jnp.float32
        ) + offset
        slope = jax.nn.sigmoid(logits)
        if own:
            down = lax.broadcasted_iota(jnp.int32, slope.shape, 0)
            along = lax.broadcasted_iota(jnp.int32, slope.shape, 1)
            slope = slope - jnp.where(down == along, 1.0, 0.0)
        return jnp.dot(
            slope.astype(jnp.bfloat16), theirs, preferred_element_type=jnp.float32
        )

    def blocks(side, first, end):
        return emb[side, first:end].reshape((end - first) * rows, emb.shape[3])

    copies["sib early"].wait_recv()
    own_sum[EARLY] = pull(emb[EARLY, OWN], blocks(LATE, OWN, AWAY), own=True)
    copies["sib late"].wait_recv()
    own_sum[LATE] = pull(emb[LATE, OWN], blocks(EARLY, OWN, AWAY), own=True)

    copies["raw"].wait_recv()
    emb[EARLY, AWAY, raw_span] = embed(away_feats[raw_span], EARLY)[0].astype(jnp.bfloat16)
    send(
        "relay raw", emb.at[EARLY, AWAY, raw_span], emb.at[LATE, FAR, raw_span], sibling
    )
    copies["early"].wait_recv()
    send(
        "relay early", emb.at[EARLY, AWAY, emb_span], emb.at[LATE, FAR, emb_span], sibling
    )
    away_sum[EARLY] = pull(emb[EARLY, AWAY], blocks(LATE, OWN, AWAY))
    copies["relay raw"].wait_recv()
    copies["relay early"].wait_recv()
    away_sum[EARLY] += pull(emb[EARLY, AWAY], emb[LATE, FAR])

    for i, span in enumerate(late_spans):
        copies["late", i].wait_recv()
        send(("relay late", i), emb.at[LATE, AWAY, span], emb.at[EARLY, FAR, span], sibling)
        part = pull(emb[EARLY, AWAY], emb[LATE, AWAY, span])
        if i < len(late_spans) - 1:
            away_sum[EARLY] += part
        else:
            away_out[EARLY] = (away_sum[EARLY] + part).astype(jnp.bfloat16)
    for i, span in enumerate(back_spans[EARLY]):
        send(
            ("back", EARLY, i),
            away_out.at[EARLY, span],
            away_in.at[EARLY, span],
            partners[EARLY],
        )

    away_sum[LATE] = pull(emb[LATE, AWAY], blocks(EARLY, OWN, FAR))
    for i in range(len(late_spans)):
        copies["relay late", i].wait_recv()
    away_out[LATE] = (
        away_sum[LATE] + pull(emb[LATE, AWAY], emb[EARLY, FAR])
    ).astype(jnp.bfloat16)
    for i, span in enumerate(back_spans[LATE]):
        send(
            ("back", LATE, i), away_out.at[LATE, span], away_in.at[LATE, span], partners[LATE]
        )

    own_sum[EARLY] += pull(emb[EARLY, OWN], blocks(LATE, AWAY, FAR + 1))
    own_sum[LATE] += pull(emb[LATE, OWN], blocks(EARLY, AWAY, FAR + 1))
    early_proj_t[...] = proj[EARLY].T
    late_proj_t[...] = proj[LATE].T

    for side in range(2):
        for i, span in enumerate(back_spans[side]):
            copies["back", side, i].wait_recv()
            slope = temper * (own_sum[side, span] + away_in[side, span].astype(jnp.float32))
            normal = unit[side, span]
            inner = jnp.sum(normal * slope, axis=1, keepdims=True)
            down = (recip[side, span] * (slope - normal * inner)).astype(jnp.bfloat16)
            if side == LATE and i == len(back_spans[side]) - 1:
                last[...] = down
            else:
                done[side, span] = jnp.dot(
                    down,
                    (early_proj_t if side == EARLY else late_proj_t)[...],
                    preferred_element_type=jnp.float32,
                )

    for copy in copies.values():
        copy.wait_send()


def finish(axis_sizes, done, last, late_proj_t, image_grad, text_grad, tail, sem):
    role = lax.rem(place_of(axis_sizes)[0], 2)
    rows = done.shape[1]
    head, end = pl.ds(0, rows - last.shape[0]), pl.ds(rows - last.shape[0], last.shape[0])

    def puts(early_grad, late_grad):
        return (
            pltpu.make_async_copy(done.at[EARLY], early_grad, sem.at[0]),
            pltpu.make_async_copy(done.at[LATE, head], late_grad.at[head], sem.at[1]),
            pltpu.make_async_copy(tail, late_grad.at[end], sem.at[2]),
        )

    for which, grads in enumerate(((text_grad, image_grad), (image_grad, text_grad))):

        @pl.when(role == which)
        def _():
            for copy in puts(*grads)[:2]:
                copy.start()

    tail[...] = jnp.dot(last[...], late_proj_t[...], preferred_element_type=jnp.float32)
    for which, grads in enumerate(((text_grad, image_grad), (image_grad, text_grad))):

        @pl.when(role == which)
        def _():
            puts(*grads)[2].start()

    for copy in puts(text_grad, image_grad):
        copy.wait()


def on_device(axis_sizes, image_feats, text_feats, image_proj, text_proj, scale, bias):
    rows, width = image_feats.shape
    embed = image_proj.shape[1]
    f32, bf16 = jnp.float32, jnp.bfloat16
    hbm = pl.BlockSpec(memory_space=pltpu.HBM)
    vmem = pl.BlockSpec(memory_space=pltpu.VMEM)
    end = spans_of(rows, LATE_BACK)[-1][1]
    n_copies = 6 + 2 * len(LATE_PARTS) + len(EARLY_BACK) + len(LATE_BACK)
    done, last, late_proj_t = pl.pallas_call(
        functools.partial(kernel, axis_sizes),
        out_shape=(
            pltpu.VMEM((2, rows, width), f32),
            pltpu.VMEM((end, embed), bf16),
            pltpu.VMEM((embed, width), bf16),
        ),
        in_specs=[hbm] * 6,
        out_specs=(vmem,) * 3,
        scratch_shapes=[
            pltpu.VMEM((2, rows, width), bf16),
            pltpu.VMEM((rows, width), bf16),
            pltpu.VMEM((2, width, embed), bf16),
            pltpu.VMEM((embed, width), bf16),
            pltpu.VMEM((2, 4, rows, embed), bf16),
            pltpu.VMEM((2, rows, embed), f32),
            pltpu.VMEM((2, rows, 1), f32),
            pltpu.VMEM((2, rows, embed), f32),
            pltpu.VMEM((2, rows, embed), f32),
            pltpu.VMEM((2, rows, embed), bf16),
            pltpu.VMEM((2, rows, embed), bf16),
            pltpu.SMEM((1,), f32),
            pltpu.SMEM((1,), f32),
            pltpu.SemaphoreType.DMA((3, 2)),
            pltpu.SemaphoreType.DMA((n_copies,)),
            pltpu.SemaphoreType.DMA((n_copies,)),
        ],
        compiler_params=pltpu.CompilerParams(
            collective_id=0, has_side_effects=True, vmem_limit_bytes=36700160
        ),
    )(
        *(
            pltpu.with_memory_space_constraint(x, pltpu.HBM)
            for x in (image_feats, text_feats, image_proj, text_proj)
        ),
        scale,
        bias,
    )
    out = jax.ShapeDtypeStruct((rows, width), f32)
    return pl.pallas_call(
        functools.partial(finish, axis_sizes),
        out_shape=(out, out),
        in_specs=[vmem] * 3,
        out_specs=(hbm, hbm),
        scratch_shapes=[
            pltpu.VMEM((end, width), f32),
            pltpu.SemaphoreType.DMA((3,)),
        ],
        compiler_params=pltpu.CompilerParams(vmem_limit_bytes=8388608),
    )(*(pltpu.with_memory_space_constraint(x, pltpu.VMEM) for x in (done, last, late_proj_t)))


def solution(mesh):
    in_specs = (P(("hst", "local"), None), P(("hst", "local"), None), P(), P(), P(), P())
    out_specs = (P(("hst", "local"), None), P(("hst", "local"), None))
    axis_sizes = (mesh.shape["hst"], mesh.shape["local"])
    return jax.shard_map(
        functools.partial(on_device, axis_sizes),
        mesh=mesh,
        in_specs=in_specs,
        out_specs=out_specs,
        check_vma=False,
    )
```

time: 28.6 us -> 27.8 us (0.972)
  local copies, waits for them, and re-layouts: 1.7 us -> 0 us
  Pallas kernels: 24.7 us -> 25.7 us
    unnamed x2 -> x0, local copies, waits for them, and re-layouts: 1.63 us -> none
    pallas_call x1 -> x2, Pallas kernels: 24.7 us -> 25.7 us  [the longest x1 24.2 us: on_device(): pl.pallas_call(functools.partial(kernel, axis_sizes), out_shape=(pltpu.VM...]
where the time goes in v1:
time: 27.8 us; the launch traced here: 27.6 us
  Pallas kernels  25.7 us (92%)
  between operations  1.93 us (7%)
    pallas_call x1, Pallas kernels, on_device(): pl.pallas_call(functools.partial(kernel, axis_sizes), out_shape=(pltpu.VM...  24.2 us
    pallas_call x1, Pallas kernels, on_device(): pl.pallas_call(functools.partial(finish, axis_sizes), out_shape=(out, out...  1.48 us

profile of v1, /device:TPU:0, one launch (start us, length us, event | category | flops | bytes accessed | tf_op | source)
XLA Modules:
  0.0 27.6 jit_solution(9207848686024383158)
XLA Ops:
  1.9 24.2 %shard_map.77 = (f32[2,128,1152]{2,1,0:T(8,128)S(1)}, bf16[32,1152]{1,0:T(8,128)(2,1)S(1)}, bf16[1152,1152]{1,0:T(8,128)(2,1)S(1)}) custom-call(bf16[128,1152]{1,0:T(8,128)(2,1)} %image_feats.1, bf16[128,1152]{1,0:T(8,128)(2,1)} %text_feats.1, bf16[1152,1152]{1,0:T(8,128)(2,1)} %image_proj.1, bf16[1152,1152]{1,0:T(8,128)(2,1)} %text_proj.1, ...), custom_call_target="tpu_custom_call" | custom-call | tf_op jit(solution)/shard_map/pallas_call | solution.py:301
  26.1 1.5 %shard_map.78 = (f32[128,1152]{1,0:T(8,128)}, f32[128,1152]{1,0:T(8,128)}) custom-call(f32[2,128,1152]{2,1,0:T(8,128)S(1)} %get-tuple-element.5.done, bf16[32,1152]{1,0:T(8,128)(2,1)S(1)} %get-tuple-element.6.last, bf16[1152,1152]{1,0:T(8,128)(2,1)S(1)} %get-tuple-element.7.late_proj_t), custom_call_target="tpu_custom_call" | custom-call | tf_op jit(solution)/shard_map/pallas_call | solution.py:340

commit v2 on v1

--- a/solution.py
+++ b/solution.py
@@ -9,11 +9,11 @@
 
 GROUP_DEVS = 8
 EARLY, LATE = 0, 1
-OWN, SIB, AWAY, FAR = range(4)
+OWN, SIB, FAR, AWAY = range(4)
 RAW_PART = (1, 2)
 LATE_PARTS = (2, 1, 1)
 EARLY_BACK = (1, 1)
-LATE_BACK = (2, 1, 1)
+LATE_BACK = (3, 1)
 
 
 def flipped(member, bit):
@@ -190,9 +190,9 @@
         return emb[side, first:end].reshape((end - first) * rows, emb.shape[3])
 
     copies["sib early"].wait_recv()
-    own_sum[EARLY] = pull(emb[EARLY, OWN], blocks(LATE, OWN, AWAY), own=True)
+    own_sum[EARLY] = pull(emb[EARLY, OWN], blocks(LATE, OWN, FAR), own=True)
     copies["sib late"].wait_recv()
-    own_sum[LATE] = pull(emb[LATE, OWN], blocks(EARLY, OWN, AWAY), own=True)
+    own_sum[LATE] = pull(emb[LATE, OWN], blocks(EARLY, OWN, FAR), own=True)
 
     copies["raw"].wait_recv()
     emb[EARLY, AWAY, raw_span] = embed(away_feats[raw_span], EARLY)[0].astype(jnp.bfloat16)
@@ -203,19 +203,15 @@
     send(
         "relay early", emb.at[EARLY, AWAY, emb_span], emb.at[LATE, FAR, emb_span], sibling
     )
-    away_sum[EARLY] = pull(emb[EARLY, AWAY], blocks(LATE, OWN, AWAY))
-    copies["relay raw"].wait_recv()
-    copies["relay early"].wait_recv()
-    away_sum[EARLY] += pull(emb[EARLY, AWAY], emb[LATE, FAR])
-
+    away_sum[...] = pull(emb[EARLY, AWAY], blocks(LATE, OWN, FAR))
     for i, span in enumerate(late_spans):
         copies["late", i].wait_recv()
         send(("relay late", i), emb.at[LATE, AWAY, span], emb.at[EARLY, FAR, span], sibling)
-        part = pull(emb[EARLY, AWAY], emb[LATE, AWAY, span])
-        if i < len(late_spans) - 1:
-            away_sum[EARLY] += part
-        else:
-            away_out[EARLY] = (away_sum[EARLY] + part).astype(jnp.bfloat16)
+    copies["relay raw"].wait_recv()
+    copies["relay early"].wait_recv()
+    away_out[EARLY] = (
+        away_sum[...] + pull(emb[EARLY, AWAY], blocks(LATE, FAR, AWAY + 1))
+    ).astype(jnp.bfloat16)
     for i, span in enumerate(back_spans[EARLY]):
         send(
             ("back", EARLY, i),
@@ -224,37 +220,39 @@
             partners[EARLY],
         )
 
-    away_sum[LATE] = pull(emb[LATE, AWAY], blocks(EARLY, OWN, FAR))
     for i in range(len(late_spans)):
         copies["relay late", i].wait_recv()
-    away_out[LATE] = (
-        away_sum[LATE] + pull(emb[LATE, AWAY], emb[EARLY, FAR])
-    ).astype(jnp.bfloat16)
+    away_out[LATE] = pull(emb[LATE, AWAY], blocks(EARLY, OWN, AWAY + 1)).astype(jnp.bfloat16)
     for i, span in enumerate(back_spans[LATE]):
         send(
             ("back", LATE, i), away_out.at[LATE, span], away_in.at[LATE, span], partners[LATE]
         )
 
-    own_sum[EARLY] += pull(emb[EARLY, OWN], blocks(LATE, AWAY, FAR + 1))
-    own_sum[LATE] += pull(emb[LATE, OWN], blocks(EARLY, AWAY, FAR + 1))
+    own_sum[EARLY] += pull(emb[EARLY, OWN], blocks(LATE, FAR, AWAY + 1))
+    own_sum[LATE] += pull(emb[LATE, OWN], blocks(EARLY, FAR, AWAY + 1))
     early_proj_t[...] = proj[EARLY].T
     late_proj_t[...] = proj[LATE].T
 
-    for side in range(2):
-        for i, span in enumerate(back_spans[side]):
-            copies["back", side, i].wait_recv()
-            slope = temper * (own_sum[side, span] + away_in[side, span].astype(jnp.float32))
-            normal = unit[side, span]
-            inner = jnp.sum(normal * slope, axis=1, keepdims=True)
-            down = (recip[side, span] * (slope - normal * inner)).astype(jnp.bfloat16)
-            if side == LATE and i == len(back_spans[side]) - 1:
-                last[...] = down
-            else:
-                done[side, span] = jnp.dot(
-                    down,
-                    (early_proj_t if side == EARLY else late_proj_t)[...],
-                    preferred_element_type=jnp.float32,
-                )
+    def down_of(side, span):
+        slope = temper * (own_sum[side, span] + away_in[side, span].astype(jnp.float32))
+        normal = unit[side, span]
+        inner = jnp.sum(normal * slope, axis=1, keepdims=True)
+        return (recip[side, span] * (slope - normal * inner)).astype(jnp.bfloat16)
+
+    for i in range(len(back_spans[EARLY])):
+        copies["back", EARLY, i].wait_recv()
+    done[EARLY] = jnp.dot(
+        down_of(EARLY, whole), early_proj_t[...], preferred_element_type=jnp.float32
+    )
+    for i, span in enumerate(back_spans[LATE]):
+        copies["back", LATE, i].wait_recv()
+        down = down_of(LATE, span)
+        if i < len(back_spans[LATE]) - 1:
+            done[LATE, span] = jnp.dot(
+                down, late_proj_t[...], preferred_element_type=jnp.float32
+            )
+        else:
+            last[...] = down
 
     for copy in copies.values():
         copy.wait_send()
@@ -279,7 +277,10 @@
             for copy in puts(*grads)[:2]:
                 copy.start()
 
-    tail[...] = jnp.dot(last[...], late_proj_t[...], preferred_element_type=jnp.float32)
+    @pl.when(role >= 0)
+    def _():
+        tail[...] = jnp.dot(last[...], late_proj_t[...], preferred_element_type=jnp.float32)
+
     for which, grads in enumerate(((text_grad, image_grad), (image_grad, text_grad))):
 
         @pl.when(role == which)
@@ -316,7 +317,7 @@
             pltpu.VMEM((2, rows, embed), f32),
             pltpu.VMEM((2, rows, 1), f32),
             pltpu.VMEM((2, rows, embed), f32),
-            pltpu.VMEM((2, rows, embed), f32),
+            pltpu.VMEM((rows, embed), f32),
             pltpu.VMEM((2, rows, embed), bf16),
             pltpu.VMEM((2, rows, embed), bf16),
             pltpu.SMEM((1,), f32),

time: 27.8 us -> 26.2 us (0.942)
  Pallas kernels: 25.7 us -> 24.1 us
    pallas_call x1, Pallas kernels: 24.2 us -> 22.8 us  [on_device(): pl.pallas_call(functools.partial(kernel, axis_sizes), out_shape=(pltpu.VM...]
where the time goes in v2:
time: 26.2 us; the launch traced here: 26 us
  Pallas kernels  24.1 us (92%)
  between operations  1.93 us (7%)
    pallas_call x1, Pallas kernels, on_device(): pl.pallas_call(functools.partial(kernel, axis_sizes), out_shape=(pltpu.VM...  22.8 us
    pallas_call x1, Pallas kernels, on_device(): pl.pallas_call(functools.partial(finish, axis_sizes), out_shape=(out, out...  1.28 us

profile of v2, /device:TPU:0, one launch (start us, length us, event | category | flops | bytes accessed | tf_op | source)
XLA Modules:
  0.0 26.0 jit_solution(16070378816975648191)
XLA Ops:
  1.9 22.8 %shard_map.77 = (f32[2,128,1152]{2,1,0:T(8,128)S(1)}, bf16[32,1152]{1,0:T(8,128)(2,1)S(1)}, bf16[1152,1152]{1,0:T(8,128)(2,1)S(1)}) custom-call(bf16[128,1152]{1,0:T(8,128)(2,1)} %image_feats.1, bf16[128,1152]{1,0:T(8,128)(2,1)} %text_feats.1, bf16[1152,1152]{1,0:T(8,128)(2,1)} %image_proj.1, bf16[1152,1152]{1,0:T(8,128)(2,1)} %text_proj.1, ...), custom_call_target="tpu_custom_call" | custom-call | tf_op jit(solution)/shard_map/pallas_call | solution.py:302
  24.7 1.3 %shard_map.78 = (f32[128,1152]{1,0:T(8,128)}, f32[128,1152]{1,0:T(8,128)}) custom-call(f32[2,128,1152]{2,1,0:T(8,128)S(1)} %get-tuple-element.5.done, bf16[32,1152]{1,0:T(8,128)(2,1)S(1)} %get-tuple-element.6.last, bf16[1152,1152]{1,0:T(8,128)(2,1)S(1)} %get-tuple-element.7.late_proj_t), custom_call_target="tpu_custom_call" | custom-call | tf_op jit(solution)/shard_map/pallas_call | solution.py:341

commit v3 on v2

--- a/solution.py
+++ b/solution.py
@@ -189,11 +189,6 @@
     def blocks(side, first, end):
         return emb[side, first:end].reshape((end - first) * rows, emb.shape[3])
 
-    copies["sib early"].wait_recv()
-    own_sum[EARLY] = pull(emb[EARLY, OWN], blocks(LATE, OWN, FAR), own=True)
-    copies["sib late"].wait_recv()
-    own_sum[LATE] = pull(emb[LATE, OWN], blocks(EARLY, OWN, FAR), own=True)
-
     copies["raw"].wait_recv()
     emb[EARLY, AWAY, raw_span] = embed(away_feats[raw_span], EARLY)[0].astype(jnp.bfloat16)
     send(
@@ -203,6 +198,7 @@
     send(
         "relay early", emb.at[EARLY, AWAY, emb_span], emb.at[LATE, FAR, emb_span], sibling
     )
+    copies["sib early"].wait_recv()
     away_sum[...] = pull(emb[EARLY, AWAY], blocks(LATE, OWN, FAR))
     for i, span in enumerate(late_spans):
         copies["late", i].wait_recv()
@@ -220,6 +216,7 @@
             partners[EARLY],
         )
 
+    copies["sib late"].wait_recv()
     for i in range(len(late_spans)):
         copies["relay late", i].wait_recv()
     away_out[LATE] = pull(emb[LATE, AWAY], blocks(EARLY, OWN, AWAY + 1)).astype(jnp.bfloat16)
@@ -228,8 +225,8 @@
             ("back", LATE, i), away_out.at[LATE, span], away_in.at[LATE, span], partners[LATE]
         )
 
-    own_sum[EARLY] += pull(emb[EARLY, OWN], blocks(LATE, FAR, AWAY + 1))
-    own_sum[LATE] += pull(emb[LATE, OWN], blocks(EARLY, FAR, AWAY + 1))
+    for side in range(2):
+        own_sum[side] = pull(emb[side, OWN], blocks(1 - side, OWN, AWAY + 1), own=True)
     early_proj_t[...] = proj[EARLY].T
     late_proj_t[...] = proj[LATE].T
 

time: 26.2 us -> 26.2 us (level)
  no operation moved by 1% of the time
where the time goes in v3:
time: 26.2 us; the launch traced here: 26 us
  Pallas kernels  24.1 us (92%)
  between operations  1.93 us (7%)
    pallas_call x1, Pallas kernels, on_device(): pl.pallas_call(functools.partial(kernel, axis_sizes), out_shape=(pltpu.VM...  22.8 us
    pallas_call x1, Pallas kernels, on_device(): pl.pallas_call(functools.partial(finish, axis_sizes), out_shape=(out, out...  1.28 us

profile of v3, /device:TPU:0, one launch (start us, length us, event | category | flops | bytes accessed | tf_op | source)
XLA Modules:
  0.0 26.0 jit_solution(4953197474641092850)
XLA Ops:
  1.9 22.8 %shard_map.77 = (f32[2,128,1152]{2,1,0:T(8,128)S(1)}, bf16[32,1152]{1,0:T(8,128)(2,1)S(1)}, bf16[1152,1152]{1,0:T(8,128)(2,1)S(1)}) custom-call(bf16[128,1152]{1,0:T(8,128)(2,1)} %image_feats.1, bf16[128,1152]{1,0:T(8,128)(2,1)} %text_feats.1, bf16[1152,1152]{1,0:T(8,128)(2,1)} %image_proj.1, bf16[1152,1152]{1,0:T(8,128)(2,1)} %text_proj.1, ...), custom_call_target="tpu_custom_call" | custom-call | tf_op jit(solution)/shard_map/pallas_call | solution.py:299
  24.7 1.3 %shard_map.78 = (f32[128,1152]{1,0:T(8,128)}, f32[128,1152]{1,0:T(8,128)}) custom-call(f32[2,128,1152]{2,1,0:T(8,128)S(1)} %get-tuple-element.5.done, bf16[32,1152]{1,0:T(8,128)(2,1)S(1)} %get-tuple-element.6.last, bf16[1152,1152]{1,0:T(8,128)(2,1)S(1)} %get-tuple-element.7.late_proj_t), custom_call_target="tpu_custom_call" | custom-call | tf_op jit(solution)/shard_map/pallas_call | solution.py:338
